TPU v7x, 128 devices: a whole 4x4x4 slice. The times are simulated.
128 devices in a mesh: comp: 2 (over core), tile: 64 (over z, y, x).
Axes of the slice: x: 4, y: 4, z: 4, core: 2. Of those that a mesh axis runs over, the one named last changes fastest.
Arguments:
- state: float32 [2, 8, 1024, 1024], P('comp', None, 'tile'), may hold values from -80 to 80, as said below
- basis: bfloat16 [12, 2, 8, 1024, 1024], P(None, 'comp', None, 'tile'), may hold values from -4 to 4
- kappa: float32 [2, 1024, 1024], P('comp', 'tile'), may hold values from 0.05 to 0.22
- vmix: float32 [2, 8, 8], P('comp'), may hold values from -1 to 1
- land_mask: int32 [1024, 1024], P('tile'), may hold values 0 or 1
- send_rows: int32 [2, 64, 64, 8], P('comp', 'tile'), may hold values from 0 to 127
- recv_slots: int32 [2, 64, 128, 4], P('comp', 'tile'), may hold values from 0 to 511
- recv_weights: float32 [2, 64, 128, 4], P('comp', 'tile'), may hold values from 0.1 to 0.4
Outputs:
- direction: float32 [2, 8, 1024, 1024], P('comp', None, 'tile')
- coefs: float32 [12], replicated
Inputs may be any that keep to these rules, and one draw needn't show every extreme that they name: `state`: the perturbation is noise plus a combination of the basis vectors.
All inputs are finite; a program needn't handle non-finite values. No bound on the sum of `land_mask` on one device may be relied on, other than what follows from the above.
Results may differ from a plain program's by a relative error of at most 0.0003.
Values sent between devices are 32-bit elements; how exact they have to be, the bound alone decides.
A program may use at most 64 MiB of HBM per device.

v0:
```python
import jax
import jax.numpy as jnp
from jax import lax
from jax.sharding import PartitionSpec as P

FLUX = 4
VECS = 12


def extended(cells, sides, width):
    for axis, dim in sides:
        count = lax.axis_size(axis)
        ends = count - 1
        head = lax.slice_in_dim(cells, 0, width, axis=dim)
        tail = lax.slice_in_dim(cells, cells.shape[dim] - width, cells.shape[dim], axis=dim)
        cells = jnp.concatenate(
            [
                lax.ppermute(tail, axis, [(i, (i + 1) % count) for i in range(ends)]),
                cells,
                lax.ppermute(head, axis, [((i + 1) % count, i) for i in range(ends)]),
            ],
            axis=dim,
        )
    return cells


def from_partner(block, axis, stride):
    count = lax.axis_size(axis)
    route = []
    for low in range(count):
        high = low | 1 << stride
        if high != low and high < count:
            route += [(low, high), (high, low)]
    return lax.ppermute(block, axis, route)


def advance(x, kap, vert_mat, maskf, forced):
    padded = extended(x, (("tile", 1),), 1)
    lap = padded[:, 2:] + padded[:, :-2] + jnp.roll(x, 1, -1) + jnp.roll(x, -1, -1) - 4.0 * x
    vert = jnp.einsum("lm,mrq->lrq", vert_mat, x, precision=lax.Precision.HIGHEST)
    return maskf * (x + kap * lap + vert + forced)


def body(state, basis, kappa, vmix, land_mask, send_rows, recv_slots, recv_weights):
    comp_id = lax.axis_index("comp")
    x = state[0]
    levels, rows, cols = x.shape
    nblk = rows * cols // 128
    surface = x[:FLUX].reshape(FLUX, nblk, 128)
    bucket = surface[:, send_rows[0, 0]]
    moved = lax.all_to_all(bucket, "tile", split_axis=1, concat_axis=1, tiled=True)
    arrived = from_partner(moved, "comp", 0)
    flat = arrived.reshape(FLUX, -1, 128)
    picked = flat[:, recv_slots[0, 0]]
    imported = jnp.einsum(
        "ek,fekq->feq", recv_weights[0, 0], picked, precision=lax.Precision.HIGHEST
    )
    imported = imported.reshape(FLUX, rows, cols)
    forced = jnp.concatenate([imported, jnp.zeros((levels - FLUX, rows, cols), jnp.float32)], 0)
    maskf = jnp.where(comp_id == 0, land_mask.astype(jnp.float32), jnp.float32(1.0))
    for step in range(2):
        x = advance(x, kappa[0], vmix[0], maskf, forced)
    total = float(levels * rows * cols * lax.axis_size("comp") * lax.axis_size("tile"))
    vflat = x.reshape(-1)
    qmat = basis[:, 0].reshape(VECS, -1)
    local_dots = jnp.dot(
        qmat, vflat, precision=lax.Precision.HIGHEST, preferred_element_type=jnp.float32
    )
    dots = lax.psum(local_dots, ("comp", "tile"))
    coefs = dots / total
    remain = vflat - jnp.dot(
        coefs, qmat, precision=lax.Precision.HIGHEST, preferred_element_type=jnp.float32
    )
    normsq = lax.psum(jnp.sum(remain * remain), ("comp", "tile"))
    direction = remain / jnp.sqrt(normsq / total + 1e-06)
    return (direction.reshape(1, levels, rows, cols), coefs)


def solution(mesh):
    return jax.shard_map(
        body,
        mesh=mesh,
        in_specs=(
            P("comp", None, "tile", None),
            P(None, "comp", None, "tile", None),
            P("comp", "tile", None),
            P("comp", None, None),
            P("tile", None),
            P("comp", "tile", None, None),
            P("comp", "tile", None, None),
            P("comp", "tile", None, None),
        ),
        out_specs=(P("comp", None, "tile", None), P()),
        check_vma=False,
    )
```

profile of v0, /device:TPU:1, one launch (start us, length us, event | category | flops | bytes accessed | tf_op | source)
XLA Modules:
  0.0 204.8 jit_solution(5193275752972541004)
XLA Ops:
  0.6 0.0 copy-start
  0.6 0.0 copy-start.1
  0.7 0.0 copy-start.4
  0.7 0.0 copy-start.3
  0.7 0.7 compare_select_fusion
  1.4 0.1 copy.16
  1.5 0.1 reshape.85
  1.6 1.0 slice.68
  2.6 0.2 copy.17
  2.8 2.6 %gather_fusion = f32[512,4,128]{2,1,0:T(4,128)} fusion(f32[4,128,128]{2,0,1:T(4,128)S(1)} %copy.17, s32[1024]{0:T(1024)S(1)} %pad_clamp_fusion.1), kind=kCustom, calls=%fused_computation | custom fusion | bytes 2099200 | tf_op jit(solution)/shard_map/gather | solution.py:50
  5.5 12.0 %all-to-all-start = ((f32[4,64,8,128]{3,0,2,1:T(4,128)}), f32[4,64,8,128]{3,0,2,1:T(4,128)S(1)}, u32[]{:S(2)}, u32[]{:S(2)}) async-start(f32[4,64,8,128]{3,0,2,1:T(4,128)} %bitcast.6), calls=%async_computation | async-start | bytes 2097152 | tf_op jit(solution)/shard_map/all_to_all | solution.py:51
  17.4 0.3 copy.28
  17.8 1.3 collective-permute-start
  19.1 4.6 %collective-permute-start.1 = (f32[8,1,1024]{2,0,1:T(8,128)S(1)}, f32[8,1,1024]{2,0,1:T(8,128)}, u32[]{:S(2)}, u32[]{:S(2)}) collective-permute-start(f32[8,1,1024]{2,0,1:T(8,128)S(1)} %get-tuple-element.15), channel_id=1, source_target_pairs={{0,1},{1,2},{2,3},{3,4},{4,5},{5,6},{6,7},{7,8},{8,9},{9,10},{10,1... | collective-permute-start | bytes 98312 | tf_op jit(solution)/shard_map/ppermute | solution.py:18
  23.7 11.4 %all-to-all-done = f32[4,64,8,128]{3,0,2,1:T(4,128)S(1)} async-done(((f32[4,64,8,128]{3,0,2,1:T(4,128)}), f32[4,64,8,128]{3,0,2,1:T(4,128)S(1)}, u32[]{:S(2)}, u32[]{:S(2)}) %all-to-all-start) | async-done | bytes 1048608 | tf_op jit(solution)/shard_map/all_to_all | solution.py:51
  35.0 2.6 %collective-permute-start.2 = (f32[4,64,8,128]{3,0,2,1:T(4,128)S(1)}, f32[4,64,8,128]{3,0,2,1:T(4,128)S(1)}, u32[]{:S(2)}, u32[]{:S(2)}) collective-permute-start(f32[4,64,8,128]{3,0,2,1:T(4,128)S(1)} %all-to-all-done), channel_id=1, source_target_pairs={{0,64},{64,0},{1,65},{65,1},{2,66},{66,2},{3,67},{67,3},{4,68},{68... | collective-permute-start | bytes 3145736 | tf_op jit(solution)/shard_map/ppermute | solution.py:34
  37.6 0.0 copy-done.4
  37.6 0.1 copy.18
  37.7 0.1 reshape.93
  37.9 0.1 copy.21
  38.0 2.3 %pad.27 = bf16[16,128,1024]{2,1,0:T(8,128)(2,1)S(1)} pad(bf16[12,128,1024]{2,1,0:T(8,128)(2,1)} %bitcast.71, bf16[]{:T(256)} %constant.52), padding=0_4x0_0x0_0 | pad | bytes 7340034
  40.3 0.0 copy-start.2
  40.3 4.3 %copy.24 = bf16[2,8,128,1024]{3,1,2,0:T(8,128)(2,1)} copy(bf16[2,8,128,1024]{3,2,1,0:T(8,128)(2,1)S(1)} %bitcast.64) | data formatting | bytes 8388608
  44.6 0.0 copy-done.2
  44.6 0.1 fusion.27
  44.7 0.9 fusion.26
  45.7 0.0 collective-permute-done.2
  45.7 2.1 %gather_fusion.1 = f32[512,4,128]{2,1,0:T(4,128)S(1)} fusion(f32[4,512,128]{2,0,1:T(4,128)S(1)} %bitcast.74, s32[1024]{0:T(1024)S(1)} %pad_clamp_fusion), kind=kCustom, calls=%fused_computation.1 | custom fusion | bytes 2099200 | tf_op jit(solution)/shard_map/gather | solution.py:54
  47.7 2.0 fusion.5
  49.8 0.0 collective-permute-done
  49.8 0.0 collective-permute-done.1
  49.8 2.0 fusion.4
  51.8 0.2 fusion.23
  52.0 1.3 collective-permute-start.3
  53.3 4.2 %collective-permute-start.4 = (f32[8,1,1024]{2,0,1:T(8,128)S(1)}, f32[8,1,1024]{2,0,1:T(8,128)S(1)}, u32[]{:S(2)}, u32[]{:S(2)}) collective-permute-start(f32[8,1,1024]{2,0,1:T(8,128)S(1)} %get-tuple-element.9), channel_id=1, source_target_pairs={{0,1},{1,2},{2,3},{3,4},{4,5},{5,6},{6,7},{7,8},{8,9},{9,10},{10,1... | collective-permute-start | bytes 98312 | tf_op jit(solution)/shard_map/ppermute | solution.py:18
  57.5 0.1 fusion.24
  57.5 0.0 collective-permute-done.3
  57.6 0.7 collective-permute-done.4
  58.3 0.9 fusion.2
  59.2 0.3 copy.19
  59.5 0.6 reshape.104
  60.1 6.5 %convolution_bitcast_fusion.1 = f32[12]{0:T(128)S(1)} fusion(f32[131072,1]{0,1:T(1,128)S(1)} %reshape.104, bf16[12,131072]{1,0:T(8,128)(2,1)} %bitcast.62), kind=kOutput, calls=%fused_computation.9 | convolution fusion | flops 18874368 | bytes 3670064 | tf_op jit(solution)/shard_map/dot_general | solution.py:66
  66.6 0.1 copy.23
  66.7 68.6 %psum.14 = f32[12]{0:T(128)S(1)} all-reduce(f32[12]{0:T(128)S(1)} %convolution_bitcast_fusion.1), channel_id=1, replica_groups=mesh['comp'=2,'tile'=64] {'comp','tile'}, use_global_device_ids=true, to_apply=%region_0.1 | all-reduce | flops 12 | bytes 96 | tf_op jit(solution)/shard_map/psum | solution.py:69
  135.3 4.0 %fusion.21 = f32[1,131072]{1,0:T(1,128)S(1)} fusion(bf16[12,131072]{1,0:T(8,128)(2,1)} %bitcast.63, f32[12]{0:T(128)S(1)} %broadcast_multiply_fusion), kind=kOutput, calls=%fused_computation.38 | convolution fusion | flops 18874368 | bytes 3670064 | tf_op jit(solution)/shard_map/dot_general | solution.py:71
  139.3 0.8 multiply_reduce_fusion
  140.1 63.1 %psum.15 = f32[]{:T(128)} all-reduce(f32[]{:T(128)} %get-tuple-element.2), channel_id=1, replica_groups=mesh['comp'=2,'tile'=64] {'comp','tile'}, use_global_device_ids=true, to_apply=%region_2.3 | all-reduce | flops 1 | bytes 8 | tf_op jit(solution)/shard_map/psum | solution.py:74
  203.9 0.9 reshape.82
  (16 shorter events, 0.1 us)
Async XLA Ops:
  0.6 49.2 %copy-start = (f32[1,8,8]{2,1,0:T(8,128)S(1)}, f32[1,8,8]{2,1,0:T(8,128)}, u32[]{:S(2)}) copy-start(f32[1,8,8]{2,1,0:T(8,128)} %param.11) | copy-start | bytes 772
  0.6 16.8 %copy-start.1 = (f32[1,8,16,1024]{3,2,1,0:T(8,128)S(1)}, f32[1,8,16,1024]{3,2,1,0:T(8,128)}, u32[]{:S(2)}) copy-start(f32[1,8,16,1024]{3,2,1,0:T(8,128)} %param.8) | copy-start | bytes 1572868
  0.7 37.0 %copy-start.4 = (s32[1,1,128,4]{2,3,1,0:T(4,128)S(1)}, s32[1,1,128,4]{2,3,1,0:T(4,128)}, u32[]{:S(2)}) copy-start(s32[1,1,128,4]{2,3,1,0:T(4,128)} %param.14) | copy-start | bytes 6148
  0.7 37.2 %copy-start.3 = (f32[1,1,128,4]{2,3,1,0:T(4,128)S(1)}, f32[1,1,128,4]{2,3,1,0:T(4,128)}, u32[]{:S(2)}) copy-start(f32[1,1,128,4]{2,3,1,0:T(4,128)} %param.15) | copy-start | bytes 6148
  5.5 29.6 %all-to-all-start = ((f32[4,64,8,128]{3,0,2,1:T(4,128)}), f32[4,64,8,128]{3,0,2,1:T(4,128)S(1)}, u32[]{:S(2)}, u32[]{:S(2)}) async-start(f32[4,64,8,128]{3,0,2,1:T(4,128)} %bitcast.6), calls=%async_computation | async-start | bytes 2097152 | tf_op jit(solution)/shard_map/all_to_all | solution.py:51
  17.8 32.0 %collective-permute-start = (f32[8,1,1024]{2,0,1:T(8,128)S(1)}, f32[8,1,1024]{2,0,1:T(8,128)}, u32[]{:S(2)}, u32[]{:S(2)}) collective-permute-start(f32[8,1,1024]{2,0,1:T(8,128)S(1)} %get-tuple-element.14), channel_id=1, source_target_pairs={{1,0},{2,1},{3,2},{4,3},{5,4},{6,5},{7,6},{8,7},{9,8},{10,9},{11,1... | collective-permute-start | bytes 98312 | tf_op jit(solution)/shard_map/ppermute | solution.py:20
  19.1 30.7 %collective-permute-start.1 = (f32[8,1,1024]{2,0,1:T(8,128)S(1)}, f32[8,1,1024]{2,0,1:T(8,128)}, u32[]{:S(2)}, u32[]{:S(2)}) collective-permute-start(f32[8,1,1024]{2,0,1:T(8,128)S(1)} %get-tuple-element.15), channel_id=1, source_target_pairs={{0,1},{1,2},{2,3},{3,4},{4,5},{5,6},{6,7},{7,8},{8,9},{9,10},{10,1... | collective-permute-start | bytes 98312 | tf_op jit(solution)/shard_map/ppermute | solution.py:18
  35.0 10.6 %collective-permute-start.2 = (f32[4,64,8,128]{3,0,2,1:T(4,128)S(1)}, f32[4,64,8,128]{3,0,2,1:T(4,128)S(1)}, u32[]{:S(2)}, u32[]{:S(2)}) collective-permute-start(f32[4,64,8,128]{3,0,2,1:T(4,128)S(1)} %all-to-all-done), channel_id=1, source_target_pairs={{0,64},{64,0},{1,65},{65,1},{2,66},{66,2},{3,67},{67,3},{4,68},{68... | collective-permute-start | bytes 3145736 | tf_op jit(solution)/shard_map/ppermute | solution.py:34
  40.3 4.3 %copy-start.2 = (s32[16,1024]{1,0:T(8,128)S(1)}, s32[16,1024]{1,0:T(8,128)}, u32[]{:S(2)}) copy-start(s32[16,1024]{1,0:T(8,128)} %param.12) | copy-start | bytes 196612
  44.6 5.2 %copy-start.6 = (f32[1,16,1024]{2,1,0:T(8,128)S(1)}, f32[1,16,1024]{2,1,0:T(8,128)}, u32[]{:S(2)}) copy-start(f32[1,16,1024]{2,1,0:T(8,128)} %param.10) | copy-start | bytes 196612
  52.0 5.6 %collective-permute-start.3 = (f32[8,1,1024]{2,0,1:T(8,128)S(1)}, f32[8,1,1024]{2,0,1:T(8,128)S(1)}, u32[]{:S(2)}, u32[]{:S(2)}) collective-permute-start(f32[8,1,1024]{2,0,1:T(8,128)S(1)} %get-tuple-element.8), channel_id=1, source_target_pairs={{1,0},{2,1},{3,2},{4,3},{5,4},{6,5},{7,6},{8,7},{9,8},{10,9},{11,1... | collective-permute-start | bytes 98312 | tf_op jit(solution)/shard_map/ppermute | solution.py:20
  53.3 5.0 %collective-permute-start.4 = (f32[8,1,1024]{2,0,1:T(8,128)S(1)}, f32[8,1,1024]{2,0,1:T(8,128)S(1)}, u32[]{:S(2)}, u32[]{:S(2)}) collective-permute-start(f32[8,1,1024]{2,0,1:T(8,128)S(1)} %get-tuple-element.9), channel_id=1, source_target_pairs={{0,1},{1,2},{2,3},{3,4},{4,5},{5,6},{6,7},{7,8},{8,9},{9,10},{10,1... | collective-permute-start | bytes 98312 | tf_op jit(solution)/shard_map/ppermute | solution.py:18
  135.3 68.6 %copy-start.5 = (f32[12]{0:T(128)}, f32[12]{0:T(128)S(1)}, u32[]{:S(2)}) copy-start(f32[12]{0:T(128)S(1)} %broadcast_multiply_fusion) | copy-start | bytes 148
where the time goes:
time: 205 us
  blocking collectives  132 us (64%)
  starting transfers between devices  25.9 us (13%)
  local copies, waits for them, and re-layouts  16.6 us (8%)
  matrix products  15.3 us (7%)
  waiting for transfers between devices  12.1 us (6%)
    psum x1, blocking collectives, body(): dots = lax.psum(local_dots, ('comp', 'tile'))  68.6 us
    psum x1, blocking collectives, body(): normsq = lax.psum(jnp.sum(remain * remain), ('comp', 'tile'))  63.1 us
    all_to_all x1, starting transfers between devices, body(): lax.all_to_all(bucket, 'tile', split_axis=1, concat_axis=1, tiled=True)  12 us
    all_to_all x1, waiting for transfers between devices, body(): lax.all_to_all(bucket, 'tile', split_axis=1, concat_axis=1, tiled=True)  11.4 us
    ppermute x2, starting transfers between devices, extended(): lax.ppermute(tail, axis, [(i, (i + 1) % count) for i in range(ends)])  8.77 us
    unnamed x18, local copies, waits for them, and re-layouts  7.05 us
    dot_general x1, matrix products, body(): jnp.dot(qmat, vflat, precision=lax.Precision.HIGHEST, preferred_element_t...  6.49 us
  transfers between devices with their start and end apart: 6, of which 2 were waited for; matrix products, arithmetic and copies ran while one was open for 6% of the time, Pallas kernels for 0%

commit v1 on v0

--- a/solution.py
+++ b/solution.py
@@ -48,7 +48,10 @@
     nblk = rows * cols // 128
     surface = x[:FLUX].reshape(FLUX, nblk, 128)
     bucket = surface[:, send_rows[0, 0]]
-    moved = lax.all_to_all(bucket, "tile", split_axis=1, concat_axis=1, tiled=True)
+    moved = jnp.concatenate(
+        lax.all_to_all(jnp.stack(jnp.split(bucket, lax.axis_size("tile"), axis=1)), "tile", 0, 0),
+        axis=1,
+    )
     arrived = from_partner(moved, "comp", 0)
     flat = arrived.reshape(FLUX, -1, 128)
     picked = flat[:, recv_slots[0, 0]]

time: 205 us -> 244 us (1.19)
  local copies, waits for them, and re-layouts: 16.6 us -> 55.3 us
    unnamed x18 -> x81, local copies, waits for them, and re-layouts: 7.05 us -> 44.9 us
  transfers between devices with their start and end apart: 6 -> 6, of which waited for: 2 -> 2; matrix products, arithmetic and copies ran while one was open for 6% -> 5% of each run, Pallas kernels for 0% -> 0%
where the time goes in v1:
time: 244 us
  blocking collectives  132 us (54%)
  local copies, waits for them, and re-layouts  55.3 us (23%)
  starting transfers between devices  26 us (11%)
  matrix products  15.4 us (6%)
  waiting for transfers between devices  12.1 us (5%)
    psum x1, blocking collectives, body(): dots = lax.psum(local_dots, ('comp', 'tile'))  68.6 us
    psum x1, blocking collectives, body(): normsq = lax.psum(jnp.sum(remain * remain), ('comp', 'tile'))  63.1 us
    unnamed x81, local copies, waits for them, and re-layouts  44.9 us
    all_to_all x1, starting transfers between devices, body(): lax.all_to_all(jnp.stack(jnp.split(bucket, lax.axis_size('tile'), axis=1)...  12 us
    all_to_all x1, waiting for transfers between devices, body(): lax.all_to_all(jnp.stack(jnp.split(bucket, lax.axis_size('tile'), axis=1)...  11.4 us
    ppermute x2, starting transfers between devices, extended(): lax.ppermute(tail, axis, [(i, (i + 1) % count) for i in range(ends)])  8.77 us
    dot_general x1, matrix products, body(): jnp.dot(qmat, vflat, precision=lax.Precision.HIGHEST, preferred_element_t...  6.49 us
  transfers between devices with their start and end apart: 6, of which 2 were waited for; matrix products, arithmetic and copies ran while one was open for 5% of the time, Pallas kernels for 0%

profile of v1, /device:TPU:1, one launch (start us, length us, event | category | flops | bytes accessed | tf_op | source)
XLA Modules:
  0.0 243.6 jit_solution(10547662754552178123)
XLA Ops:
  0.6 0.7 compare_select_fusion
  1.5 1.0 slice.68
  2.8 2.1 gather_fusion
  5.5 0.6 constant_dynamic-update-slice_fusion.62
  7.9 0.6 constant_dynamic-update-slice_fusion.58
  8.5 0.6 constant_dynamic-update-slice_fusion.57
  10.3 0.6 constant_dynamic-update-slice_fusion.54
  11.5 0.6 constant_dynamic-update-slice_fusion.52
  12.7 0.6 constant_dynamic-update-slice_fusion.50
  13.9 0.6 constant_dynamic-update-slice_fusion.48
  16.9 0.6 constant_dynamic-update-slice_fusion.43
  17.5 0.6 constant_dynamic-update-slice_fusion.42
  18.2 0.6 constant_dynamic-update-slice_fusion.41
  19.4 0.6 constant_dynamic-update-slice_fusion.39
  22.9 0.6 constant_dynamic-update-slice_fusion.33
  28.3 0.6 constant_dynamic-update-slice_fusion.24
  29.5 0.6 constant_dynamic-update-slice_fusion.22
  30.1 0.6 constant_dynamic-update-slice_fusion.21
  31.3 0.6 constant_dynamic-update-slice_fusion.19
  33.7 0.6 constant_dynamic-update-slice_fusion.15
  34.4 0.6 constant_dynamic-update-slice_fusion.14
  37.4 0.6 constant_dynamic-update-slice_fusion.9
  38.0 0.6 constant_dynamic-update-slice_fusion.8
  39.2 0.6 constant_dynamic-update-slice_fusion.6
  42.2 0.6 constant_dynamic-update-slice_fusion.1
  43.4 12.0 %all-to-all-start = ((f32[64,4,1,8,128]{4,3,1,2,0:T(8,128)}), f32[64,4,1,8,128]{4,3,1,2,0:T(8,128)S(1)}, u32[]{:S(2)}, u32[]{:S(2)}) async-start(f32[64,4,1,8,128]{4,3,1,2,0:T(8,128)} %constant_dynamic-update-slice_fusion), calls=%async_computation | async-start | bytes 2097152 | tf_op jit(solution)/shard_map/all_to_all | solution.py:52
  55.7 1.3 collective-permute-start
  57.0 4.6 %collective-permute-start.1 = (f32[8,1,1024]{2,0,1:T(8,128)S(1)}, f32[8,1,1024]{2,0,1:T(8,128)}, u32[]{:S(2)}, u32[]{:S(2)}) collective-permute-start(f32[8,1,1024]{2,0,1:T(8,128)S(1)} %get-tuple-element.15), channel_id=1, source_target_pairs={{0,1},{1,2},{2,3},{3,4},{4,5},{5,6},{6,7},{7,8},{8,9},{9,10},{10,1... | collective-permute-start | bytes 98312 | tf_op jit(solution)/shard_map/ppermute | solution.py:18
  61.6 11.4 %all-to-all-done = f32[64,4,1,8,128]{4,3,1,2,0:T(8,128)S(1)} async-done(((f32[64,4,1,8,128]{4,3,1,2,0:T(8,128)}), f32[64,4,1,8,128]{4,3,1,2,0:T(8,128)S(1)}, u32[]{:S(2)}, u32[]{:S(2)}) %all-to-all-start) | async-done | bytes 1048608 | tf_op jit(solution)/shard_map/all_to_all | solution.py:52
  73.1 2.7 %collective-permute-start.2 = (f32[4,64,8,128]{3,2,1,0:T(8,128)S(1)}, f32[4,64,8,128]{3,2,1,0:T(8,128)S(1)}, u32[]{:S(2)}, u32[]{:S(2)}) collective-permute-start(f32[4,64,8,128]{3,2,1,0:T(8,128)S(1)} %bitcast.401), channel_id=1, source_target_pairs={{0,64},{64,0},{1,65},{65,1},{2,66},{66,2},{3,67},{67,3},{4,68},{68... | collective-permute-start | bytes 3145736 | tf_op jit(solution)/shard_map/ppermute | solution.py:34
  76.1 2.3 pad.27
  78.4 4.3 %copy.225 = bf16[2,8,128,1024]{3,1,2,0:T(8,128)(2,1)} copy(bf16[2,8,128,1024]{3,2,1,0:T(8,128)(2,1)S(1)} %bitcast.326) | data formatting | bytes 8388608
  82.8 0.9 fusion.26
  83.8 0.7 copy.219
  84.4 2.1 gather_fusion.1
  86.5 2.0 fusion.5
  88.6 2.0 fusion.4
  90.8 1.3 collective-permute-start.3
  92.1 4.2 %collective-permute-start.4 = (f32[8,1,1024]{2,0,1:T(8,128)S(1)}, f32[8,1,1024]{2,0,1:T(8,128)S(1)}, u32[]{:S(2)}, u32[]{:S(2)}) collective-permute-start(f32[8,1,1024]{2,0,1:T(8,128)S(1)} %get-tuple-element.9), channel_id=1, source_target_pairs={{0,1},{1,2},{2,3},{3,4},{4,5},{5,6},{6,7},{7,8},{8,9},{9,10},{10,1... | collective-permute-start | bytes 98312 | tf_op jit(solution)/shard_map/ppermute | solution.py:18
  96.3 0.7 collective-permute-done.4
  97.1 0.9 fusion.2
  98.3 0.6 reshape.112
  98.9 6.5 %convolution_bitcast_fusion.1 = f32[12]{0:T(128)S(1)} fusion(f32[131072,1]{0,1:T(1,128)S(1)} %reshape.112, bf16[12,131072]{1,0:T(8,128)(2,1)} %bitcast.324), kind=kOutput, calls=%fused_computation.9 | convolution fusion | flops 18874368 | bytes 3670064 | tf_op jit(solution)/shard_map/dot_general | solution.py:69
  105.5 68.6 %psum.14 = f32[12]{0:T(128)S(1)} all-reduce(f32[12]{0:T(128)S(1)} %convolution_bitcast_fusion.1), channel_id=1, replica_groups=mesh['comp'=2,'tile'=64] {'comp','tile'}, use_global_device_ids=true, to_apply=%region_0.1 | all-reduce | flops 12 | bytes 96 | tf_op jit(solution)/shard_map/psum | solution.py:72
  174.1 4.0 %fusion.21 = f32[1,131072]{1,0:T(1,128)S(1)} fusion(bf16[12,131072]{1,0:T(8,128)(2,1)} %bitcast.325, f32[12]{0:T(128)S(1)} %broadcast_multiply_fusion), kind=kOutput, calls=%fused_computation.168 | convolution fusion | flops 18874368 | bytes 3670064 | tf_op jit(solution)/shard_map/dot_general | solution.py:74
  178.1 0.8 multiply_reduce_fusion
  178.8 63.1 %psum.15 = f32[]{:T(128)} all-reduce(f32[]{:T(128)} %get-tuple-element.2), channel_id=1, replica_groups=mesh['comp'=2,'tile'=64] {'comp','tile'}, use_global_device_ids=true, to_apply=%region_2.3 | all-reduce | flops 1 | bytes 8 | tf_op jit(solution)/shard_map/psum | solution.py:77
  242.7 0.9 reshape.90
  (83 shorter events, 27.2 us)
Async XLA Ops:
  0.6 87.9 %copy-start = (f32[1,8,8]{2,1,0:T(8,128)S(1)}, f32[1,8,8]{2,1,0:T(8,128)}, u32[]{:S(2)}) copy-start(f32[1,8,8]{2,1,0:T(8,128)} %param.11) | copy-start | bytes 772
  2.7 52.6 %copy-start.1 = (f32[1,8,16,1024]{3,2,1,0:T(8,128)S(1)}, f32[1,8,16,1024]{3,2,1,0:T(8,128)}, u32[]{:S(2)}) copy-start(f32[1,8,16,1024]{3,2,1,0:T(8,128)} %param.8) | copy-start | bytes 1572868
  4.9 70.8 %copy-start.4 = (s32[1,1,128,4]{2,3,1,0:T(4,128)S(1)}, s32[1,1,128,4]{2,3,1,0:T(4,128)}, u32[]{:S(2)}) copy-start(s32[1,1,128,4]{2,3,1,0:T(4,128)} %param.14) | copy-start | bytes 6148
  4.9 71.0 %copy-start.3 = (f32[1,1,128,4]{2,3,1,0:T(4,128)S(1)}, f32[1,1,128,4]{2,3,1,0:T(4,128)}, u32[]{:S(2)}) copy-start(f32[1,1,128,4]{2,3,1,0:T(4,128)} %param.15) | copy-start | bytes 6148
  43.4 29.6 %all-to-all-start = ((f32[64,4,1,8,128]{4,3,1,2,0:T(8,128)}), f32[64,4,1,8,128]{4,3,1,2,0:T(8,128)S(1)}, u32[]{:S(2)}, u32[]{:S(2)}) async-start(f32[64,4,1,8,128]{4,3,1,2,0:T(8,128)} %constant_dynamic-update-slice_fusion), calls=%async_computation | async-start | bytes 2097152 | tf_op jit(solution)/shard_map/all_to_all | solution.py:52
  55.7 32.8 %collective-permute-start = (f32[8,1,1024]{2,0,1:T(8,128)S(1)}, f32[8,1,1024]{2,0,1:T(8,128)}, u32[]{:S(2)}, u32[]{:S(2)}) collective-permute-start(f32[8,1,1024]{2,0,1:T(8,128)S(1)} %get-tuple-element.14), channel_id=1, source_target_pairs={{1,0},{2,1},{3,2},{4,3},{5,4},{6,5},{7,6},{8,7},{9,8},{10,9},{11,1... | collective-permute-start | bytes 98312 | tf_op jit(solution)/shard_map/ppermute | solution.py:20
  57.0 31.5 %collective-permute-start.1 = (f32[8,1,1024]{2,0,1:T(8,128)S(1)}, f32[8,1,1024]{2,0,1:T(8,128)}, u32[]{:S(2)}, u32[]{:S(2)}) collective-permute-start(f32[8,1,1024]{2,0,1:T(8,128)S(1)} %get-tuple-element.15), channel_id=1, source_target_pairs={{0,1},{1,2},{2,3},{3,4},{4,5},{5,6},{6,7},{7,8},{8,9},{9,10},{10,1... | collective-permute-start | bytes 98312 | tf_op jit(solution)/shard_map/ppermute | solution.py:18
  73.1 10.7 %collective-permute-start.2 = (f32[4,64,8,128]{3,2,1,0:T(8,128)S(1)}, f32[4,64,8,128]{3,2,1,0:T(8,128)S(1)}, u32[]{:S(2)}, u32[]{:S(2)}) collective-permute-start(f32[4,64,8,128]{3,2,1,0:T(8,128)S(1)} %bitcast.401), channel_id=1, source_target_pairs={{0,64},{64,0},{1,65},{65,1},{2,66},{66,2},{3,67},{67,3},{4,68},{68... | collective-permute-start | bytes 3145736 | tf_op jit(solution)/shard_map/ppermute | solution.py:34
  78.4 4.3 %copy-start.2 = (s32[16,1024]{1,0:T(8,128)S(1)}, s32[16,1024]{1,0:T(8,128)}, u32[]{:S(2)}) copy-start(s32[16,1024]{1,0:T(8,128)} %param.12) | copy-start | bytes 196612
  82.7 5.9 %copy-start.6 = (f32[1,16,1024]{2,1,0:T(8,128)S(1)}, f32[1,16,1024]{2,1,0:T(8,128)}, u32[]{:S(2)}) copy-start(f32[1,16,1024]{2,1,0:T(8,128)} %param.10) | copy-start | bytes 196612
  90.8 5.6 %collective-permute-start.3 = (f32[8,1,1024]{2,0,1:T(8,128)S(1)}, f32[8,1,1024]{2,0,1:T(8,128)S(1)}, u32[]{:S(2)}, u32[]{:S(2)}) collective-permute-start(f32[8,1,1024]{2,0,1:T(8,128)S(1)} %get-tuple-element.8), channel_id=1, source_target_pairs={{1,0},{2,1},{3,2},{4,3},{5,4},{6,5},{7,6},{8,7},{9,8},{10,9},{11,1... | collective-permute-start | bytes 98312 | tf_op jit(solution)/shard_map/ppermute | solution.py:20
  92.1 5.0 %collective-permute-start.4 = (f32[8,1,1024]{2,0,1:T(8,128)S(1)}, f32[8,1,1024]{2,0,1:T(8,128)S(1)}, u32[]{:S(2)}, u32[]{:S(2)}) collective-permute-start(f32[8,1,1024]{2,0,1:T(8,128)S(1)} %get-tuple-element.9), channel_id=1, source_target_pairs={{0,1},{1,2},{2,3},{3,4},{4,5},{5,6},{6,7},{7,8},{8,9},{9,10},{10,1... | collective-permute-start | bytes 98312 | tf_op jit(solution)/shard_map/ppermute | solution.py:18
  174.1 68.6 %copy-start.5 = (f32[12]{0:T(128)}, f32[12]{0:T(128)S(1)}, u32[]{:S(2)}) copy-start(f32[12]{0:T(128)S(1)} %broadcast_multiply_fusion) | copy-start | bytes 148
